TPU v7x, 128 devices: a whole 4x4x4 slice. The times are simulated.
128 devices in a mesh: blk: 32 (over x, y, z_lo), segment: 4 (over z_hi, core).
Axes of the slice: x: 4, y: 4, z: 4 (z_hi: 2, z_lo: 2; z = z_hi * 2 + z_lo), core: 2. Of those that a mesh axis runs over, the one named last changes fastest.
Arguments:
- latent_queries: bfloat16 [2, 128, 2048], P(None, 'blk'), may hold values from -400 to 400
- latent_embed: bfloat16 [2, 128, 2048], P(None, 'blk'), may hold values from -6 to 6
- history_keys: bfloat16 [2, 32768, 2048], P(None, ('blk', 'segment')), may hold values from -6 to 6
- history_values: bfloat16 [2, 32768, 2048], P(None, ('blk', 'segment')), may hold values from -7 to 7
- latent_pos: int32 [2, 128], replicated, may hold values from 1 to 32768, as said below
- norm_gain: float32 [4, 2048], P('segment'), may hold values from 0.25 to 1.75
- w_qkv: bfloat16 [4, 2048, 3, 2048], P('segment', None, None, 'blk'), may hold values from -0.125 to 0.125
- w_out: bfloat16 [4, 2048, 2048], P('segment', 'blk'), may hold values from -0.125 to 0.125
Outputs:
- latents_out: float32 [2, 128, 2048], P(None, 'blk', 'segment')
Inputs may be any that keep to these rules, and one draw needn't show every extreme that they name: `latent_pos`: Non-decreasing along the latents of a micro-batch; latent i sees at least (i + 1) * 256 positions and the last latent sees all 32768.
All inputs are finite; a program needn't handle non-finite values.
Results may differ from a plain program's by a relative error of at most 0.0085.
Values may be sent and summed in bfloat16 or wider, within the bound.
A program may use at most 64 MiB of HBM per device.

v0:
```python
import jax
import jax.numpy as jnp
from jax import lax
from jax.sharding import PartitionSpec as P

HEADS = 16
epsilon = 1e-06
masked = -1e30


def from_partner(array, axis, distance):
    return lax.ppermute(array, axis, [(i, i ^ 1 << distance) for i in range(lax.axis_size(axis))])


def shifted(value, axis, steps):
    count = lax.axis_size(axis)
    first, last = (max(0, -steps), min(count, count - steps))
    return lax.ppermute(value, axis, [(source, source + steps) for source in range(first, last)])


def normalize(latent_state, gain_row):
    factor = lax.rsqrt(jnp.mean(latent_state * latent_state, axis=1, keepdims=True) + epsilon)
    return (latent_state * factor * gain_row).astype(jnp.bfloat16)


def attend_columns(mixed_qkv, head_size):
    lat_count = mixed_qkv.shape[0]
    columns = mixed_qkv.shape[1] // 3
    head_span = min(columns, head_size)
    head_groups = columns // head_span
    query_part = mixed_qkv[:, :columns].reshape(lat_count, head_groups, head_span)
    key_part = mixed_qkv[:, columns : 2 * columns].reshape(lat_count, head_groups, head_span)
    value_part = mixed_qkv[:, 2 * columns :].reshape(lat_count, head_groups, head_span)
    scores = jnp.einsum("ipd,jpd->pij", query_part, key_part, preferred_element_type=jnp.float32)
    scores = scores + from_partner(scores, "blk", 0)
    scores = scores * head_size ** (-0.5)
    row_ids = lax.broadcasted_iota(jnp.int32, (lat_count, lat_count), 0)
    col_ids = lax.broadcasted_iota(jnp.int32, (lat_count, lat_count), 1)
    scores = jnp.where((col_ids <= row_ids)[None], scores, masked)
    row_top = jnp.max(scores, axis=2, keepdims=True)
    weights = jnp.exp(scores - row_top)
    soft_weights = (weights / jnp.sum(weights, axis=2, keepdims=True)).astype(jnp.bfloat16)
    attended = jnp.einsum(
        "pij,jpd->ipd", soft_weights, value_part, preferred_element_type=jnp.float32
    )
    return attended.reshape(lat_count, columns).astype(jnp.bfloat16)


def layer_full(latent_state, gain_row, projection, output_rows, head_size):
    normed = normalize(latent_state, gain_row)
    mixed_qkv = jnp.dot(normed, projection, preferred_element_type=jnp.float32).astype(jnp.bfloat16)
    attended = attend_columns(mixed_qkv, head_size)
    update = jnp.dot(attended, output_rows, preferred_element_type=jnp.float32)
    return latent_state + lax.psum(update, "blk")


def on_device(
    latent_queries, latent_embed, history_keys, history_values, latent_pos, norm_gain, w_qkv, w_out
):
    segment_count = lax.axis_size("segment")
    blk_id = lax.axis_index("blk")
    segment_id = lax.axis_index("segment")
    micro_count = history_keys.shape[0]
    hist_rows = history_keys.shape[1]
    width = history_keys.shape[2]
    head_size = width // HEADS
    gathered = lax.all_gather(latent_queries, "blk", axis=1, tiled=True)
    lat_count = gathered.shape[1]
    first_key = (blk_id * segment_count + segment_id) * hist_rows
    key_ids = first_key + jnp.arange(hist_rows, dtype=jnp.int32)
    visible = (key_ids[None, None, :] < latent_pos[:, :, None])[:, None]
    query_heads = gathered.reshape(micro_count, lat_count, HEADS, head_size)
    key_heads = history_keys.reshape(micro_count, hist_rows, HEADS, head_size)
    value_heads = history_values.reshape(micro_count, hist_rows, HEADS, head_size)
    scores = jnp.einsum(
        "mqhd,mkhd->mhqk", query_heads, key_heads, preferred_element_type=jnp.float32
    ) * head_size ** (-0.5)
    scores = jnp.where(visible, scores, masked)
    highest = lax.pmax(jnp.max(scores, axis=3), ("blk", "segment"))
    weights = jnp.where(visible, jnp.exp(scores - highest[..., None]), 0.0)
    totals = jnp.transpose(jnp.sum(weights, axis=3), (0, 2, 1))
    partial_value = jnp.einsum(
        "mhqk,mkhd->mqhd",
        weights.astype(jnp.bfloat16),
        value_heads,
        preferred_element_type=jnp.float32,
    )
    partial_value = partial_value.reshape(micro_count, lat_count, width)
    summed, counted = (
        lax.psum_scatter(partial_value, "blk", scatter_dimension=1, tiled=True),
        lax.psum_scatter(totals, "blk", scatter_dimension=1, tiled=True),
    )
    summed, counted = lax.psum((summed, counted), "segment")
    rows_here = summed.shape[1]
    attended = (
        summed.reshape(micro_count, rows_here, HEADS, head_size) / counted[..., None]
    ).reshape(micro_count, rows_here, width)
    start_state = latent_embed.astype(jnp.float32) + attended
    gain_row = norm_gain[0]
    projection = w_qkv[0].reshape(width, -1)
    output_rows = w_out[0]
    tower_in = lax.all_gather(start_state, "blk", axis=1, tiled=True)
    rounds = micro_count + segment_count - 1
    last_segment = segment_count - 1
    incoming = jnp.zeros_like(tower_in[0])
    finished = []
    for round_index in range(rounds):
        if round_index < micro_count:
            incoming = jnp.where(segment_id == 0, tower_in[round_index], incoming)
        latent_state = layer_full(incoming, gain_row, projection, output_rows, head_size)
        if round_index >= last_segment:
            finished.append(jnp.where(segment_id == last_segment, latent_state, 0.0))
        if round_index + 1 < rounds:
            incoming = shifted(latent_state, "segment", 1)
    results = jnp.stack(finished)
    own_rows = latent_embed.shape[1]
    results = lax.dynamic_slice_in_dim(results, blk_id * own_rows, own_rows, 1)
    return lax.psum_scatter(results, "segment", scatter_dimension=2, tiled=True)


def solution(mesh):
    return jax.shard_map(
        on_device,
        mesh=mesh,
        in_specs=(
            P(None, "blk", None),
            P(None, "blk", None),
            P(None, ("blk", "segment"), None),
            P(None, ("blk", "segment"), None),
            P(),
            P("segment", None),
            P("segment", None, None, "blk"),
            P("segment", "blk", None),
        ),
        out_specs=P(None, "blk", "segment"),
        check_vma=False,
    )
```

profile of v0, /device:TPU:1, one launch (start us, length us, event | category | flops | bytes accessed | tf_op | source)
XLA Modules:
  0.0 2481.4 jit_solution(8695598158295302768)
XLA Ops:
  6.5 1.6 copy.17
  8.2 4.0 copy.28
  12.3 127.7 %all-gather.3.cloned.1.call-done = bf16[2,128,2048]{2,0,1:T(2,128)(2,1)} async-done(((bf16[2,4,2048]{2,0,1:T(2,128)(2,1)}), bf16[2,128,2048]{2,0,1:T(2,128)(2,1)}) %all-gather.3.cloned.1.call-update) | async-done | bytes 1048592 | tf_op jit(solution)/shard_map/all_gather | solution.py:67
  139.9 3.7 copy.18
  143.6 4.4 fusion
  148.0 87.3 %pmax.7 = f32[2,16,128]{2,1,0:T(8,128)S(1)} all-reduce(f32[2,16,128]{2,1,0:T(8,128)S(1)} %get-tuple-element.11), channel_id=1, replica_groups=mesh['blk'=32,'segment'=4] {'blk','segment'}, use_global_device_ids=true, to_apply=%region_1.2 | all-reduce | flops 4096 | bytes 32768 | tf_op jit(solution)/shard_map/pmax | solution.py:79
  235.3 5.4 fusion.3
  240.7 2.9 copy.22
  243.7 0.6 dynamic-slice
  245.0 3.1 fusion.1
  248.2 131.5 %all-reduce.1 = f32[2,128,16]{2,1,0:T(8,128)S(1)} all-reduce(f32[2,128,16]{2,1,0:T(8,128)S(1)} %copy.23), channel_id=3, replica_groups=mesh['blk'=32,'segment'=4] {'blk'}, use_global_device_ids=true, to_apply=%region_5.6.clone | all-reduce | flops 4096 | bytes 32768
  379.8 153.2 %all-reduce.22.cloned.1.call-done = f32[2,128,2048]{2,1,0:T(8,128)} async-done(((f32[2,128,2048]{2,1,0:T(8,128)}), f32[2,128,2048]{2,1,0:T(8,128)}) %all-reduce.22.cloned.1.call-update) | async-done | bytes 2097168
  533.0 1.5 constant_dynamic-slice_fusion.1
  534.6 29.4 %psum.50 = f32[2,4,16]{2,1,0:T(4,128)S(1)} all-reduce(f32[2,4,16]{2,1,0:T(4,128)S(1)} %constant_dynamic-slice_fusion), channel_id=1, replica_groups=mesh['blk'=32,'segment'=4] {'segment'}, use_global_device_ids=true, to_apply=%region_6.7 | all-reduce | flops 128 | bytes 1024 | tf_op jit(solution)/shard_map/psum | solution.py:93
  564.2 34.6 %all-reduce.10.cloned.1.call-done = f32[2,4,2048]{2,1,0:T(4,128)} async-done(((f32[2,4,2048]{2,1,0:T(4,128)}), f32[2,4,2048]{2,1,0:T(4,128)}) %all-reduce.10.cloned.1.call-update) | async-done | bytes 65552 | tf_op jit(solution)/shard_map/psum | solution.py:93
  598.8 0.9 divide_add_fusion
  599.6 0.7 copy.24
  600.4 128.9 %all-gather.5.cloned.1.call-done = f32[2,128,2048]{2,0,1:T(2,128)} async-done(((f32[2,4,2048]{2,0,1:T(2,128)}), f32[2,128,2048]{2,0,1:T(2,128)}) %all-gather.5.cloned.1.call-update) | async-done | bytes 2097168 | tf_op jit(solution)/shard_map/all_gather | solution.py:102
  729.2 5.4 fusion.100
  735.0 0.5 copy-done.6
  735.6 0.6 convolution_convert_fusion.4
  736.4 1.4 collective-permute-start
  737.8 2.3 collective-permute-done
  740.2 1.5 fusion.14
  741.7 311.0 %all-reduce.12.cloned.1.call-done = f32[128,2048]{1,0:T(8,128)} async-done(((f32[128,2048]{1,0:T(8,128)}), f32[128,2048]{1,0:T(8,128)}) %all-reduce.12.cloned.1.call-update) | async-done | bytes 1048592 | tf_op jit(solution)/shard_map/psum | solution.py:54
  1052.8 2.0 bitcast_add_fusion
  1054.8 28.3 %collective-permute-start.1 = (f32[128,2048]{1,0:T(8,128)S(1)}, f32[128,2048]{1,0:T(8,128)S(1)}, u32[]{:S(2)}, u32[]{:S(2)}) collective-permute-start(f32[128,2048]{1,0:T(8,128)S(1)} %bitcast_add_fusion), channel_id=1, source_target_pairs={{0,1},{1,2},{2,3},{4,5},{5,6},{6,7},{8,9},{9,10},{10,11},{12,13},{... | collective-permute-start | bytes 3145736 | tf_op jit(solution)/shard_map/ppermute | solution.py:18
  1083.1 12.2 collective-permute-done.1
  1095.4 1.9 multiply_reduce_fusion.3
  1097.3 1.0 copy-done.4
  1098.2 0.5 convolution_convert_fusion.3
  1099.4 2.8 collective-permute-done.2
  1102.2 1.5 fusion.16
  1103.7 289.7 %all-reduce.14.cloned.1.call-done = f32[128,2048]{1,0:T(8,128)} async-done(((f32[128,2048]{1,0:T(8,128)}), f32[128,2048]{1,0:T(8,128)}) %all-reduce.14.cloned.1.call-update) | async-done | bytes 1048592 | tf_op jit(solution)/shard_map/psum | solution.py:54
  1393.4 1.7 add.118
  1395.1 28.1 %collective-permute-start.3 = (f32[128,2048]{1,0:T(8,128)S(1)}, f32[128,2048]{1,0:T(8,128)S(1)}, u32[]{:S(2)}, u32[]{:S(2)}) collective-permute-start(f32[128,2048]{1,0:T(8,128)S(1)} %add.118), channel_id=1, source_target_pairs={{0,1},{1,2},{2,3},{4,5},{5,6},{6,7},{8,9},{9,10},{10,11},{12,13},{... | collective-permute-start | bytes 3145736 | tf_op jit(solution)/shard_map/ppermute | solution.py:18
  1423.2 12.4 collective-permute-done.3
  1435.8 0.8 copy-done.3
  1436.6 0.5 convolution_convert_fusion.2
  1437.7 2.8 collective-permute-done.4
  1440.6 1.5 fusion.18
  1442.1 289.7 %all-reduce.16.cloned.1.call-done = f32[128,2048]{1,0:T(8,128)} async-done(((f32[128,2048]{1,0:T(8,128)}), f32[128,2048]{1,0:T(8,128)}) %all-reduce.16.cloned.1.call-update) | async-done | bytes 1048592 | tf_op jit(solution)/shard_map/psum | solution.py:54
  1731.8 1.7 add.121
  1733.5 28.1 %collective-permute-start.5 = (f32[128,2048]{1,0:T(8,128)S(1)}, f32[128,2048]{1,0:T(8,128)S(1)}, u32[]{:S(2)}, u32[]{:S(2)}) collective-permute-start(f32[128,2048]{1,0:T(8,128)S(1)} %add.121), channel_id=1, source_target_pairs={{0,1},{1,2},{2,3},{4,5},{5,6},{6,7},{8,9},{9,10},{10,11},{12,13},{... | collective-permute-start | bytes 3145736 | tf_op jit(solution)/shard_map/ppermute | solution.py:18
  1761.6 12.4 collective-permute-done.5
  1774.2 0.9 copy-done.2
  1775.1 0.5 convolution_convert_fusion.1
  1776.2 2.8 collective-permute-done.6
  1779.0 1.5 fusion.20
  1780.6 289.6 %all-reduce.18.cloned.1.call-done = f32[128,2048]{1,0:T(8,128)} async-done(((f32[128,2048]{1,0:T(8,128)}), f32[128,2048]{1,0:T(8,128)}) %all-reduce.18.cloned.1.call-update) | async-done | bytes 1048592 | tf_op jit(solution)/shard_map/psum | solution.py:54
  2070.2 2.7 select_bitcast_fusion.1
  2072.9 28.1 %collective-permute-start.7 = (f32[128,2048]{1,0:T(8,128)S(1)}, f32[128,2048]{1,0:T(8,128)S(1)}, u32[]{:S(2)}, u32[]{:S(2)}) collective-permute-start(f32[128,2048]{1,0:T(8,128)S(1)} %get-tuple-element.6), channel_id=1, source_target_pairs={{0,1},{1,2},{2,3},{4,5},{5,6},{6,7},{8,9},{9,10},{10,11},{12,13},{... | collective-permute-start | bytes 3145736 | tf_op jit(solution)/shard_map/ppermute | solution.py:18
  2101.0 12.4 collective-permute-done.7
  2113.6 0.5 convolution_convert_fusion
  2115.1 2.8 collective-permute-done.8
  2117.9 1.5 fusion.22
  2119.5 289.7 %all-reduce.20.cloned.1.call-done = f32[128,2048]{1,0:T(8,128)} async-done(((f32[128,2048]{1,0:T(8,128)}), f32[128,2048]{1,0:T(8,128)}) %all-reduce.20.cloned.1.call-update) | async-done | bytes 1048592 | tf_op jit(solution)/shard_map/psum | solution.py:54
  2409.2 1.7 select_bitcast_fusion
  2410.8 0.9 fusion.44
  2411.7 2.3 copy.33
  2414.0 3.3 reshape.239
  2417.4 55.1 %reduce-scatter.6.cloned.1.call-done = f32[512,8]{1,0:T(8,128)} async-done(((f32[2048,8]{1,0:T(8,128)}), f32[512,8]{1,0:T(8,128)}) %reduce-scatter.6.cloned.1.call-update) | async-done | bytes 16400
  2472.5 1.3 reshape.240
  2473.8 0.8 copy.34
  (74 shorter events, 5.4 us)
Async XLA Ops:
  6.5 137.1 %copy-start = (bf16[2,256,2048]{2,1,0:T(8,128)(2,1)S(1)}, bf16[2,256,2048]{2,1,0:T(8,128)(2,1)}, u32[]{:S(2)}) copy-start(bf16[2,256,2048]{2,1,0:T(8,128)(2,1)} %param.10) | copy-start | bytes 6291460
  6.5 5.6 copy-start.10
  6.5 133.4 %all-gather.3.cloned.1.call-start = ((), (), s32[]{:S(2)}) async-start(), calls=%async_computation.1 | async-start | bytes 1081344 | tf_op jit(solution)/shard_map/all_gather | solution.py:67
  8.1 524.9 %all-reduce.22.cloned.1.call-start = ((), (), s32[]{:S(2)}) async-start(), calls=%async_computation.10 | async-start | bytes 4194304
  240.7 3.0 copy-start.11
  243.6 355.1 %copy-start.9 = (bf16[2,4,2048]{2,1,0:T(4,128)(2,1)S(1)}, bf16[2,4,2048]{2,1,0:T(4,128)(2,1)}, u32[]{:S(2)}) copy-start(bf16[2,4,2048]{2,1,0:T(4,128)(2,1)} %param.9) | copy-start | bytes 98308
  243.7 355.1 %all-reduce.10.cloned.1.call-start = ((), (), s32[]{:S(2)}) async-start(), calls=%async_computation.2 | async-start | bytes 131072 | tf_op jit(solution)/shard_map/psum | solution.py:93
  248.1 487.5 %copy-start.1 = (bf16[1,2048,3,64]{1,3,2,0:T(8,128)(2,1)S(1)}, bf16[1,2048,3,64]{1,3,2,0:T(8,128)(2,1)}, u32[]{:S(2)}) copy-start(bf16[1,2048,3,64]{1,3,2,0:T(8,128)(2,1)} %param.14) | copy-start | bytes 2359300
  248.1 487.5 %copy-start.8 = (f32[1,2048]{1,0:T(1,128)S(1)}, f32[1,2048]{1,0:T(1,128)}, u32[]{:S(2)}) copy-start(f32[1,2048]{1,0:T(1,128)} %param.13) | copy-start | bytes 24580
  534.6 205.6 %copy-start.7 = (bf16[1,64,2048]{2,1,0:T(8,128)(2,1)S(1)}, bf16[1,64,2048]{2,1,0:T(8,128)(2,1)}, u32[]{:S(2)}) copy-start(bf16[1,64,2048]{2,1,0:T(8,128)(2,1)} %param.15) | copy-start | bytes 786436
  534.6 194.7 %all-gather.5.cloned.1.call-start = ((), (), s32[]{:S(2)}) async-start(), calls=%async_computation.3 | async-start | bytes 2162688 | tf_op jit(solution)/shard_map/all_gather | solution.py:102
  600.3 452.5 %all-reduce.12.cloned.1.call-start = ((), (), s32[]{:S(2)}) async-start(), calls=%async_computation.4 | async-start | bytes 2097152 | tf_op jit(solution)/shard_map/psum | solution.py:54
  734.6 1.0 copy-start.6
  736.4 3.7 collective-permute-start
  741.7 651.7 %all-reduce.14.cloned.1.call-start = ((), (), s32[]{:S(2)}) async-start(), calls=%async_computation.5 | async-start | bytes 2097152 | tf_op jit(solution)/shard_map/psum | solution.py:54
  1054.8 40.6 %collective-permute-start.1 = (f32[128,2048]{1,0:T(8,128)S(1)}, f32[128,2048]{1,0:T(8,128)S(1)}, u32[]{:S(2)}, u32[]{:S(2)}) collective-permute-start(f32[128,2048]{1,0:T(8,128)S(1)} %bitcast_add_fusion), channel_id=1, source_target_pairs={{0,1},{1,2},{2,3},{4,5},{5,6},{6,7},{8,9},{9,10},{10,11},{12,13},{... | collective-permute-start | bytes 3145736 | tf_op jit(solution)/shard_map/ppermute | solution.py:18
  1097.2 1.0 copy-start.4
  1098.9 3.2 collective-permute-start.2
  1103.7 628.1 %all-reduce.16.cloned.1.call-start = ((), (), s32[]{:S(2)}) async-start(), calls=%async_computation.6 | async-start | bytes 2097152 | tf_op jit(solution)/shard_map/psum | solution.py:54
  1395.1 40.6 %collective-permute-start.3 = (f32[128,2048]{1,0:T(8,128)S(1)}, f32[128,2048]{1,0:T(8,128)S(1)}, u32[]{:S(2)}, u32[]{:S(2)}) collective-permute-start(f32[128,2048]{1,0:T(8,128)S(1)} %add.118), channel_id=1, source_target_pairs={{0,1},{1,2},{2,3},{4,5},{5,6},{6,7},{8,9},{9,10},{10,11},{12,13},{... | collective-permute-start | bytes 3145736 | tf_op jit(solution)/shard_map/ppermute | solution.py:18
  1435.6 1.0 copy-start.3
  1437.3 3.2 collective-permute-start.4
  1442.1 628.1 %all-reduce.18.cloned.1.call-start = ((), (), s32[]{:S(2)}) async-start(), calls=%async_computation.7 | async-start | bytes 2097152 | tf_op jit(solution)/shard_map/psum | solution.py:54
  1733.5 40.6 %collective-permute-start.5 = (f32[128,2048]{1,0:T(8,128)S(1)}, f32[128,2048]{1,0:T(8,128)S(1)}, u32[]{:S(2)}, u32[]{:S(2)}) collective-permute-start(f32[128,2048]{1,0:T(8,128)S(1)} %add.121), channel_id=1, source_target_pairs={{0,1},{1,2},{2,3},{4,5},{5,6},{6,7},{8,9},{9,10},{10,11},{12,13},{... | collective-permute-start | bytes 3145736 | tf_op jit(solution)/shard_map/ppermute | solution.py:18
  1774.0 1.0 copy-start.2
  1775.7 3.2 collective-permute-start.6
  1780.5 628.7 %all-reduce.20.cloned.1.call-start = ((), (), s32[]{:S(2)}) async-start(), calls=%async_computation.8 | async-start | bytes 2097152 | tf_op jit(solution)/shard_map/psum | solution.py:54
  2072.9 40.5 %collective-permute-start.7 = (f32[128,2048]{1,0:T(8,128)S(1)}, f32[128,2048]{1,0:T(8,128)S(1)}, u32[]{:S(2)}, u32[]{:S(2)}) collective-permute-start(f32[128,2048]{1,0:T(8,128)S(1)} %get-tuple-element.6), channel_id=1, source_target_pairs={{0,1},{1,2},{2,3},{4,5},{5,6},{6,7},{8,9},{9,10},{10,11},{12,13},{... | collective-permute-start | bytes 3145736 | tf_op jit(solution)/shard_map/ppermute | solution.py:18
  2113.4 1.0 copy-start.5
  2114.7 3.2 collective-permute-start.8
  2119.4 353.1 %reduce-scatter.6.cloned.1.call-start = ((), (), s32[]{:S(2)}) async-start(), calls=%async_computation.9 | async-start | bytes 1310720
Sparse Core Ops, SparseCore 0:
  9.0 130.9 all-gather.2
  243.8 289.1 all-reduce.21
  535.5 63.2 all-reduce.9
  600.4 128.7 all-gather.4
  741.8 310.9 all-reduce.11
  1103.8 289.5 all-reduce.13
  1442.2 289.5 all-reduce.15
  1780.6 289.4 all-reduce.17
  2119.5 289.6 all-reduce.19
  2417.5 54.9 reduce-scatter.5
where the time goes:
time: 2480 us
  waiting for transfers between devices  2030 us (82%)
  blocking collectives  248 us (10%)
  starting transfers between devices  116 us (5%)
  local copies, waits for them, and re-layouts  31.8 us (1%)
    psum x5, waiting for transfers between devices, layer_full(): return latent_state + lax.psum(update, 'blk')  1470 us
    unnamed x12, waiting for transfers between devices  208 us
    unnamed x1, blocking collectives  132 us
    all_gather x1, waiting for transfers between devices, on_device(): tower_in = lax.all_gather(start_state, 'blk', axis=1, tiled=True)  129 us
    all_gather x1, waiting for transfers between devices, on_device(): gathered = lax.all_gather(latent_queries, 'blk', axis=1, tiled=True)  128 us
    ppermute x4, starting transfers between devices, shifted(): lax.ppermute(value, axis, [(source, source + steps) for source in range(f...  113 us
    pmax x1, blocking collectives, on_device(): highest = lax.pmax(jnp.max(scores, axis=3), ('blk', 'segment'))  87.3 us
  transfers between devices with their start and end apart: 19, of which 19 were waited for; matrix products, arithmetic and copies ran while one was open for 0% of the time, Pallas kernels for 0%

commit v1 on v0

--- a/solution.py
+++ b/solution.py
@@ -64,7 +64,9 @@
     hist_rows = history_keys.shape[1]
     width = history_keys.shape[2]
     head_size = width // HEADS
-    gathered = lax.all_gather(latent_queries, "blk", axis=1, tiled=True)
+    gathered = jnp.concatenate(
+        lax.all_to_all(jnp.stack([latent_queries] * lax.axis_size("blk")), "blk", 0, 0), axis=1
+    )
     lat_count = gathered.shape[1]
     first_key = (blk_id * segment_count + segment_id) * hist_rows
     key_ids = first_key + jnp.arange(hist_rows, dtype=jnp.int32)

time: 2480 us -> 2360 us (0.952)
  waiting for transfers between devices: 2030 us -> 1920 us
    all_gather x1 -> x0, waiting for transfers between devices: 128 us -> none  [on_device(): gathered = lax.all_gather(latent_queries, 'blk', axis=1, tiled=True)]
    unnamed x12 -> x11, waiting for transfers between devices: 208 us -> 210 us
where the time goes in v1:
time: 2360 us; the launch traced here: 2350 us
  waiting for transfers between devices  1920 us (81%)
  blocking collectives  224 us (9%)
  starting transfers between devices  125 us (5%)
  local copies, waits for them, and re-layouts  34.4 us (1%)
    psum x5, waiting for transfers between devices, layer_full(): return latent_state + lax.psum(update, 'blk')  1470 us
    unnamed x11, waiting for transfers between devices  210 us
    unnamed x1, blocking collectives  130 us
    all_gather x1, waiting for transfers between devices, on_device(): tower_in = lax.all_gather(start_state, 'blk', axis=1, tiled=True)  129 us
    ppermute x4, starting transfers between devices, shifted(): lax.ppermute(value, axis, [(source, source + steps) for source in range(f...  112 us
    pmax x1, blocking collectives, on_device(): highest = lax.pmax(jnp.max(scores, axis=3), ('blk', 'segment'))  64.7 us
    ppermute x4, waiting for transfers between devices, shifted(): lax.ppermute(value, axis, [(source, source + steps) for source in range(f...  49.5 us
  transfers between devices with their start and end apart: 19, of which 19 were waited for; matrix products, arithmetic and copies ran while one was open for 0% of the time, Pallas kernels for 0%

profile of v1, /device:TPU:1, one launch (start us, length us, event | category | flops | bytes accessed | tf_op | source)
XLA Modules:
  0.0 2354.2 jit_solution(15061850140836011860)
XLA Ops:
  6.5 2.5 stack.8
  9.0 9.3 all-to-all-start
  18.4 4.0 copy.25
  22.5 12.1 all-to-all-done
  34.6 2.8 copy.16
  37.4 2.5 reshape_reshape.3
  39.9 4.2 fusion
  44.1 64.7 %pmax.7 = f32[2,16,128]{2,1,0:T(8,128)S(1)} all-reduce(f32[2,16,128]{2,1,0:T(8,128)S(1)} %get-tuple-element.11), channel_id=1, replica_groups=mesh['blk'=32,'segment'=4] {'blk','segment'}, use_global_device_ids=true, to_apply=%region_1.2 | all-reduce | flops 4096 | bytes 32768 | tf_op jit(solution)/shard_map/pmax | solution.py:81
  108.8 5.4 fusion.3
  114.2 2.9 copy.20
  117.2 0.6 dynamic-slice
  118.4 3.1 fusion.1
  121.7 130.4 %all-reduce.1 = f32[2,128,16]{2,1,0:T(8,128)S(1)} all-reduce(f32[2,128,16]{2,1,0:T(8,128)S(1)} %copy.21), channel_id=3, replica_groups=mesh['blk'=32,'segment'=4] {'blk'}, use_global_device_ids=true, to_apply=%region_5.6.clone | all-reduce | flops 4096 | bytes 32768
  252.1 154.3 %all-reduce.22.cloned.1.call-done = f32[2,128,2048]{2,1,0:T(8,128)} async-done(((f32[2,128,2048]{2,1,0:T(8,128)}), f32[2,128,2048]{2,1,0:T(8,128)}) %all-reduce.22.cloned.1.call-update) | async-done | bytes 2097168
  406.4 1.5 constant_dynamic-slice_fusion.1
  408.0 29.4 %psum.50 = f32[2,4,16]{2,1,0:T(4,128)S(1)} all-reduce(f32[2,4,16]{2,1,0:T(4,128)S(1)} %constant_dynamic-slice_fusion), channel_id=1, replica_groups=mesh['blk'=32,'segment'=4] {'segment'}, use_global_device_ids=true, to_apply=%region_6.7 | all-reduce | flops 128 | bytes 1024 | tf_op jit(solution)/shard_map/psum | solution.py:95
  437.6 34.6 %all-reduce.10.cloned.1.call-done = f32[2,4,2048]{2,1,0:T(4,128)} async-done(((f32[2,4,2048]{2,1,0:T(4,128)}), f32[2,4,2048]{2,1,0:T(4,128)}) %all-reduce.10.cloned.1.call-update) | async-done | bytes 65552 | tf_op jit(solution)/shard_map/psum | solution.py:95
  472.1 0.9 divide_add_fusion
  473.0 0.7 copy.22
  473.8 128.9 %all-gather.2.cloned.1.call-done = f32[2,128,2048]{2,0,1:T(2,128)} async-done(((f32[2,4,2048]{2,0,1:T(2,128)}), f32[2,128,2048]{2,0,1:T(2,128)}) %all-gather.2.cloned.1.call-update) | async-done | bytes 2097168 | tf_op jit(solution)/shard_map/all_gather | solution.py:104
  602.7 5.4 fusion.101
  608.5 0.5 copy-done.6
  609.1 0.6 convolution_convert_fusion.4
  609.9 1.3 collective-permute-start
  611.2 2.6 collective-permute-done
  613.9 1.5 fusion.14
  615.5 310.4 %all-reduce.12.cloned.1.call-done = f32[128,2048]{1,0:T(8,128)} async-done(((f32[128,2048]{1,0:T(8,128)}), f32[128,2048]{1,0:T(8,128)}) %all-reduce.12.cloned.1.call-update) | async-done | bytes 1048592 | tf_op jit(solution)/shard_map/psum | solution.py:54
  925.9 2.0 bitcast_add_fusion
  927.9 28.3 %collective-permute-start.1 = (f32[128,2048]{1,0:T(8,128)S(1)}, f32[128,2048]{1,0:T(8,128)S(1)}, u32[]{:S(2)}, u32[]{:S(2)}) collective-permute-start(f32[128,2048]{1,0:T(8,128)S(1)} %bitcast_add_fusion), channel_id=1, source_target_pairs={{0,1},{1,2},{2,3},{4,5},{5,6},{6,7},{8,9},{9,10},{10,11},{12,13},{... | collective-permute-start | bytes 3145736 | tf_op jit(solution)/shard_map/ppermute | solution.py:18
  956.3 12.2 collective-permute-done.1
  968.5 1.9 multiply_reduce_fusion.3
  970.4 1.0 copy-done.4
  971.4 0.5 convolution_convert_fusion.3
  972.5 2.8 collective-permute-done.2
  975.3 1.5 fusion.16
  976.8 289.7 %all-reduce.14.cloned.1.call-done = f32[128,2048]{1,0:T(8,128)} async-done(((f32[128,2048]{1,0:T(8,128)}), f32[128,2048]{1,0:T(8,128)}) %all-reduce.14.cloned.1.call-update) | async-done | bytes 1048592 | tf_op jit(solution)/shard_map/psum | solution.py:54
  1266.6 1.7 add.118
  1268.2 28.1 %collective-permute-start.3 = (f32[128,2048]{1,0:T(8,128)S(1)}, f32[128,2048]{1,0:T(8,128)S(1)}, u32[]{:S(2)}, u32[]{:S(2)}) collective-permute-start(f32[128,2048]{1,0:T(8,128)S(1)} %add.118), channel_id=1, source_target_pairs={{0,1},{1,2},{2,3},{4,5},{5,6},{6,7},{8,9},{9,10},{10,11},{12,13},{... | collective-permute-start | bytes 3145736 | tf_op jit(solution)/shard_map/ppermute | solution.py:18
  1296.4 12.4 collective-permute-done.3
  1309.0 0.8 copy-done.3
  1310.9 2.8 collective-permute-done.4
  1313.7 1.5 fusion.18
  1315.3 289.6 %all-reduce.16.cloned.1.call-done = f32[128,2048]{1,0:T(8,128)} async-done(((f32[128,2048]{1,0:T(8,128)}), f32[128,2048]{1,0:T(8,128)}) %all-reduce.16.cloned.1.call-update) | async-done | bytes 1048592 | tf_op jit(solution)/shard_map/psum | solution.py:54
  1604.8 1.7 add.121
  1606.5 28.1 %collective-permute-start.5 = (f32[128,2048]{1,0:T(8,128)S(1)}, f32[128,2048]{1,0:T(8,128)S(1)}, u32[]{:S(2)}, u32[]{:S(2)}) collective-permute-start(f32[128,2048]{1,0:T(8,128)S(1)} %add.121), channel_id=1, source_target_pairs={{0,1},{1,2},{2,3},{4,5},{5,6},{6,7},{8,9},{9,10},{10,11},{12,13},{... | collective-permute-start | bytes 3145736 | tf_op jit(solution)/shard_map/ppermute | solution.py:18
  1634.6 12.4 collective-permute-done.5
  1647.2 0.9 copy-done.2
  1649.2 2.8 collective-permute-done.6
  1652.0 1.5 fusion.20
  1653.6 290.3 %all-reduce.18.cloned.1.call-done = f32[128,2048]{1,0:T(8,128)} async-done(((f32[128,2048]{1,0:T(8,128)}), f32[128,2048]{1,0:T(8,128)}) %all-reduce.18.cloned.1.call-update) | async-done | bytes 1048592 | tf_op jit(solution)/shard_map/psum | solution.py:54
  1943.8 2.7 select_bitcast_fusion.1
  1946.6 27.4 %collective-permute-start.7 = (f32[128,2048]{1,0:T(8,128)S(1)}, f32[128,2048]{1,0:T(8,128)S(1)}, u32[]{:S(2)}, u32[]{:S(2)}) collective-permute-start(f32[128,2048]{1,0:T(8,128)S(1)} %get-tuple-element.6), channel_id=1, source_target_pairs={{0,1},{1,2},{2,3},{4,5},{5,6},{6,7},{8,9},{9,10},{10,11},{12,13},{... | collective-permute-start | bytes 3145736 | tf_op jit(solution)/shard_map/ppermute | solution.py:18
  1974.0 12.4 collective-permute-done.7
  1986.6 0.5 convolution_convert_fusion
  1988.0 2.8 collective-permute-done.8
  1990.9 1.5 fusion.22
  1992.5 289.9 %all-reduce.20.cloned.1.call-done = f32[128,2048]{1,0:T(8,128)} async-done(((f32[128,2048]{1,0:T(8,128)}), f32[128,2048]{1,0:T(8,128)}) %all-reduce.20.cloned.1.call-update) | async-done | bytes 1048592 | tf_op jit(solution)/shard_map/psum | solution.py:54
  2282.4 1.7 select_bitcast_fusion
  2284.0 0.9 fusion.45
  2284.9 2.3 copy.30
  2287.2 3.3 reshape.241
  2290.6 55.0 %reduce-scatter.6.cloned.1.call-done = f32[512,8]{1,0:T(8,128)} async-done(((f32[2048,8]{1,0:T(8,128)}), f32[512,8]{1,0:T(8,128)}) %reduce-scatter.6.cloned.1.call-update) | async-done | bytes 16400
  2345.6 1.3 reshape.242
  2346.9 0.8 copy.31
  (74 shorter events, 6.3 us)
Async XLA Ops:
  6.5 33.4 %copy-start = (bf16[2,256,2048]{2,1,0:T(8,128)(2,1)S(1)}, bf16[2,256,2048]{2,1,0:T(8,128)(2,1)}, u32[]{:S(2)}) copy-start(bf16[2,256,2048]{2,1,0:T(8,128)(2,1)} %param.10) | copy-start | bytes 6291460
  6.5 15.8 copy-start.10
  9.0 25.6 %all-to-all-start = ((bf16[32,2,4,2048]{3,2,1,0:T(4,128)(2,1)}), bf16[32,2,4,2048]{3,2,1,0:T(4,128)(2,1)}, u32[]{:S(2)}, u32[]{:S(2)}) async-start(bf16[32,2,4,2048]{3,2,1,0:T(4,128)(2,1)} %stack.8), calls=%async_computation | async-start | bytes 2097152 | tf_op jit(solution)/shard_map/all_to_all | solution.py:68
  18.4 388.0 %all-reduce.22.cloned.1.call-start = ((), (), s32[]{:S(2)}) async-start(), calls=%async_computation.10 | async-start | bytes 4194304
  114.2 3.0 copy-start.11
  117.1 355.1 %copy-start.9 = (bf16[2,4,2048]{2,1,0:T(4,128)(2,1)S(1)}, bf16[2,4,2048]{2,1,0:T(4,128)(2,1)}, u32[]{:S(2)}) copy-start(bf16[2,4,2048]{2,1,0:T(4,128)(2,1)} %param.9) | copy-start | bytes 98308
  117.1 355.0 %all-reduce.10.cloned.1.call-start = ((), (), s32[]{:S(2)}) async-start(), calls=%async_computation.2 | async-start | bytes 131072 | tf_op jit(solution)/shard_map/psum | solution.py:95
  121.5 487.5 %copy-start.1 = (bf16[1,2048,3,64]{1,3,2,0:T(8,128)(2,1)S(1)}, bf16[1,2048,3,64]{1,3,2,0:T(8,128)(2,1)}, u32[]{:S(2)}) copy-start(bf16[1,2048,3,64]{1,3,2,0:T(8,128)(2,1)} %param.14) | copy-start | bytes 2359300
  121.6 487.5 %copy-start.8 = (f32[1,2048]{1,0:T(1,128)S(1)}, f32[1,2048]{1,0:T(1,128)}, u32[]{:S(2)}) copy-start(f32[1,2048]{1,0:T(1,128)} %param.13) | copy-start | bytes 24580
  408.0 206.0 %copy-start.7 = (bf16[1,64,2048]{2,1,0:T(8,128)(2,1)S(1)}, bf16[1,64,2048]{2,1,0:T(8,128)(2,1)}, u32[]{:S(2)}) copy-start(bf16[1,64,2048]{2,1,0:T(8,128)(2,1)} %param.15) | copy-start | bytes 786436
  408.0 194.7 %all-gather.2.cloned.1.call-start = ((), (), s32[]{:S(2)}) async-start(), calls=%async_computation.3 | async-start | bytes 2162688 | tf_op jit(solution)/shard_map/all_gather | solution.py:104
  473.7 452.2 %all-reduce.12.cloned.1.call-start = ((), (), s32[]{:S(2)}) async-start(), calls=%async_computation.4 | async-start | bytes 2097152 | tf_op jit(solution)/shard_map/psum | solution.py:54
  608.1 1.0 copy-start.6
  609.9 3.9 collective-permute-start
  615.4 651.1 %all-reduce.14.cloned.1.call-start = ((), (), s32[]{:S(2)}) async-start(), calls=%async_computation.5 | async-start | bytes 2097152 | tf_op jit(solution)/shard_map/psum | solution.py:54
  927.9 40.6 %collective-permute-start.1 = (f32[128,2048]{1,0:T(8,128)S(1)}, f32[128,2048]{1,0:T(8,128)S(1)}, u32[]{:S(2)}, u32[]{:S(2)}) collective-permute-start(f32[128,2048]{1,0:T(8,128)S(1)} %bitcast_add_fusion), channel_id=1, source_target_pairs={{0,1},{1,2},{2,3},{4,5},{5,6},{6,7},{8,9},{9,10},{10,11},{12,13},{... | collective-permute-start | bytes 3145736 | tf_op jit(solution)/shard_map/ppermute | solution.py:18
  970.4 1.0 copy-start.4
  972.0 3.2 collective-permute-start.2
  976.8 628.0 %all-reduce.16.cloned.1.call-start = ((), (), s32[]{:S(2)}) async-start(), calls=%async_computation.6 | async-start | bytes 2097152 | tf_op jit(solution)/shard_map/psum | solution.py:54
  1268.2 40.6 %collective-permute-start.3 = (f32[128,2048]{1,0:T(8,128)S(1)}, f32[128,2048]{1,0:T(8,128)S(1)}, u32[]{:S(2)}, u32[]{:S(2)}) collective-permute-start(f32[128,2048]{1,0:T(8,128)S(1)} %add.118), channel_id=1, source_target_pairs={{0,1},{1,2},{2,3},{4,5},{5,6},{6,7},{8,9},{9,10},{10,11},{12,13},{... | collective-permute-start | bytes 3145736 | tf_op jit(solution)/shard_map/ppermute | solution.py:18
  1308.8 1.0 copy-start.3
  1310.4 3.2 collective-permute-start.4
  1315.2 628.6 %all-reduce.18.cloned.1.call-start = ((), (), s32[]{:S(2)}) async-start(), calls=%async_computation.7 | async-start | bytes 2097152 | tf_op jit(solution)/shard_map/psum | solution.py:54
  1606.5 40.6 %collective-permute-start.5 = (f32[128,2048]{1,0:T(8,128)S(1)}, f32[128,2048]{1,0:T(8,128)S(1)}, u32[]{:S(2)}, u32[]{:S(2)}) collective-permute-start(f32[128,2048]{1,0:T(8,128)S(1)} %add.121), channel_id=1, source_target_pairs={{0,1},{1,2},{2,3},{4,5},{5,6},{6,7},{8,9},{9,10},{10,11},{12,13},{... | collective-permute-start | bytes 3145736 | tf_op jit(solution)/shard_map/ppermute | solution.py:18
  1647.0 1.0 copy-start.2
  1648.7 3.2 collective-permute-start.6
  1653.5 628.9 %all-reduce.20.cloned.1.call-start = ((), (), s32[]{:S(2)}) async-start(), calls=%async_computation.8 | async-start | bytes 2097152 | tf_op jit(solution)/shard_map/psum | solution.py:54
  1946.6 39.8 %collective-permute-start.7 = (f32[128,2048]{1,0:T(8,128)S(1)}, f32[128,2048]{1,0:T(8,128)S(1)}, u32[]{:S(2)}, u32[]{:S(2)}) collective-permute-start(f32[128,2048]{1,0:T(8,128)S(1)} %get-tuple-element.6), channel_id=1, source_target_pairs={{0,1},{1,2},{2,3},{4,5},{5,6},{6,7},{8,9},{9,10},{10,11},{12,13},{... | collective-permute-start | bytes 3145736 | tf_op jit(solution)/shard_map/ppermute | solution.py:18
  1986.4 1.0 copy-start.5
  1987.6 3.2 collective-permute-start.8
  1992.4 353.2 %reduce-scatter.6.cloned.1.call-start = ((), (), s32[]{:S(2)}) async-start(), calls=%async_computation.9 | async-start | bytes 1310720
Sparse Core Ops, SparseCore 0:
  117.2 289.1 all-reduce.21
  408.9 63.2 all-reduce.9
  473.8 128.8 all-gather.1
  615.5 310.3 all-reduce.11
  976.9 289.5 all-reduce.13
  1315.3 289.4 all-reduce.15
  1653.6 290.1 all-reduce.17
  1992.5 289.7 all-reduce.19
  2290.7 54.8 reduce-scatter.5
